TPU v7x, 32 devices: a whole 2x2x4 slice. The times are simulated.
32 devices in a mesh: dev: 32 (over z, y, x, core).
Axes of the slice: x: 2, y: 2, z: 4, core: 2. Of those that a mesh axis runs over, the one named last changes fastest.
Arguments:
- prior_labels: bfloat16 [65536, 512], P('dev'), may hold values from 0.0009994507 to 1
- label_class: int32 [65536], P('dev'), may hold values from 0 to 511
- labeled: int32 [65536], P('dev'), may hold values 0 or 1
- features: bfloat16 [65536, 1024], P('dev'), may hold values from -6 to 6
- tile_cols: int32 [512, 8], P('dev'), may hold values from 0 to 17, as said below
- tile_weights: bfloat16 [512, 8, 128, 128], P('dev'), may hold values from 0 to 1, as said below
- halo_owner: int32 [8192, 1], P('dev'), may hold values from 0 to 31; in each aligned block of 256 rows (0 to 255, 256 to 511, ...) at most 16 rows name the same one
- halo_local: int32 [8192], P('dev'), may hold values from 0 to 2047
- batch_owner: int32 [16384, 1], P('dev'), may hold values from 0 to 31; in each aligned block of 512 rows (0 to 511, 512 to 1023, ...) at most 32 rows name the same one
- batch_local: int32 [16384], P('dev'), may hold values from 0 to 2047
- w_in: bfloat16 [4096, 1024], replicated, may hold values from -0.1875 to 0.1875
- w_out: bfloat16 [4096, 512], replicated, may hold values from -0.09375 to 0.09375
Outputs:
- propagated: bfloat16 [65536, 512], P('dev')
- row_error: float32 [16384], P('dev')
- grad_in: float32 [4096, 1024], P('dev')
- grad_out: float32 [4096, 512], P('dev')
Inputs may be any that keep to these rules, and one draw needn't show every extreme that they name: `tile_cols`: in each row tile's list the first 6 entries are tiles of the device's own rows (below 16), the first of them the row tile itself; the last 2 are halo tiles (16 and above). Entries may repeat. Every halo tile of a device is listed by some row tile of that device. `tile_weights`: strictly positive. `halo_owner`: within the 256 rows of one device no owner appears more than 16 times; in some device one owner appears exactly 16 times. `batch_owner`: within the 512 rows of one device no owner appears more than 32 times; in some device one owner appears exactly 32 times.
All inputs are finite; a program needn't handle non-finite values. No bound on the sum of `labeled` on one device may be relied on, other than what follows from the above.
Results may differ from a plain program's by a relative error of at most 0.0017.
Values may be sent and summed in bfloat16 or wider, within the bound.
A program may use at most 128 MiB of HBM per device.

v0:
```python
import math

import jax
import jax.numpy as jnp
from jax import lax
from jax.sharding import PartitionSpec as P


def slot_of(owner, capacity, devices):
    matches = (owner[:, None] == jnp.arange(devices, dtype=jnp.int32)[None, :]).astype(jnp.int32)
    earlier = jnp.cumsum(matches, axis=0) - matches
    return owner * capacity + jnp.sum(earlier * matches, axis=1)


def request_table(position, local, capacity, devices):
    table = jnp.zeros((devices * capacity,), jnp.int32).at[position].set(local)
    return table.reshape(devices, capacity)


def contract_rows(left, right):
    return lax.dot_general(
        left, right, (((0,), (0,)), ((), ())), preferred_element_type=jnp.float32
    )


def contract_cols(left, right):
    return lax.dot_general(
        left, right, (((1,), (1,)), ((), ())), preferred_element_type=jnp.float32
    )


def on_device(
    prior_labels,
    label_class,
    labeled,
    features,
    tile_cols,
    tile_weights,
    halo_owner,
    halo_local,
    batch_owner,
    batch_local,
    w_in,
    w_out,
):
    devices = lax.axis_size("dev")
    node_count, classes = prior_labels.shape
    feat_width = features.shape[1]
    tile_rows = tile_weights.shape[-1]
    own_tiles = node_count // tile_rows
    halo_count = halo_owner.shape[0]
    batch_count = batch_owner.shape[0]
    halo_capacity = 2 * halo_count // devices
    batch_capacity = 2 * batch_count // devices
    halo_slot = slot_of(halo_owner[:, 0], halo_capacity, devices)
    batch_slot = slot_of(batch_owner[:, 0], batch_capacity, devices)
    halo_wanted, batch_wanted = (
        lax.all_to_all(
            request_table(halo_slot, halo_local, halo_capacity, devices),
            "dev",
            split_axis=0,
            concat_axis=0,
            tiled=True,
        ),
        lax.all_to_all(
            request_table(batch_slot, batch_local, batch_capacity, devices),
            "dev",
            split_axis=0,
            concat_axis=0,
            tiled=True,
        ),
    )
    halo_served = prior_labels[halo_wanted]
    halo_back, feature_back = (
        lax.all_to_all(halo_served, "dev", split_axis=0, concat_axis=0, tiled=True),
        lax.all_to_all(features[batch_wanted], "dev", split_axis=0, concat_axis=0, tiled=True),
    )
    halo_labels = halo_back.reshape(devices * halo_capacity, classes)[halo_slot]
    own_table = prior_labels.reshape(own_tiles, tile_rows, classes)
    halo_table = halo_labels.reshape(halo_count // tile_rows, tile_rows, classes)
    joined = jnp.concatenate([own_table, halo_table], axis=0)
    spread = jnp.einsum(
        "rkij,rkjc->ric", tile_weights, joined[tile_cols], preferred_element_type=jnp.float32
    )
    degree = jnp.sum(tile_weights, axis=(1, 3), dtype=jnp.float32)
    seeds = (
        (label_class[:, None] == jnp.arange(classes, dtype=jnp.int32)[None, :])
        & (labeled[:, None] == 1)
    ).astype(jnp.float32)
    propagated = (
        0.8 * (spread / degree[:, :, None]).reshape(node_count, classes) + 0.2 * seeds
    ).astype(jnp.bfloat16)
    label_back = lax.all_to_all(
        propagated[batch_wanted], "dev", split_axis=0, concat_axis=0, tiled=True
    )
    batch_x = feature_back.reshape(devices * batch_capacity, feat_width)[batch_slot]
    batch_z = label_back.reshape(devices * batch_capacity, classes)[batch_slot]
    log_z = jnp.log(batch_z.astype(jnp.float32))
    target = log_z - jnp.mean(log_z, axis=1, keepdims=True)
    hidden = jnp.tanh(contract_cols(batch_x, w_in)).astype(jnp.bfloat16)
    logits = jnp.dot(hidden, w_out, preferred_element_type=jnp.float32)
    differ = logits - target
    row_error = 0.5 * jnp.mean(differ * differ, axis=1)
    residue = (differ / math.sqrt(batch_count * devices)).astype(jnp.bfloat16)
    hidden_wide = hidden.astype(jnp.float32)
    back = (contract_cols(residue, w_out) * (1.0 - hidden_wide * hidden_wide)).astype(jnp.bfloat16)
    summed = lax.psum_scatter(
        jnp.concatenate([contract_rows(back, batch_x), contract_rows(hidden, residue)], axis=1),
        "dev",
        scatter_dimension=0,
        tiled=True,
    )
    grad_in = summed[:, :feat_width]
    grad_out = summed[:, feat_width:]
    return (propagated, row_error, grad_in, grad_out)


def solution(mesh):
    in_specs = (
        P("dev", None),
        P("dev"),
        P("dev"),
        P("dev", None),
        P("dev", None),
        P("dev", None, None, None),
        P("dev", None),
        P("dev"),
        P("dev", None),
        P("dev"),
        P(),
        P(),
    )
    out_specs = (P("dev", None), P("dev"), P("dev", None), P("dev", None))
    return jax.shard_map(
        on_device, mesh=mesh, in_specs=in_specs, out_specs=out_specs, check_vma=False
    )
```

profile of v0, /device:TPU:14, one launch (start us, length us, event | category | flops | bytes accessed | tf_op | source)
XLA Modules:
  0.0 468.5 jit_solution(13121985876190421877)
XLA Ops:
  7.2 0.0 copy-start.4
  7.2 0.7 fusion.13
  7.9 0.6 reduce-window.14
  8.4 0.2 slice_reduce_fusion.1
  8.7 0.8 fusion.12
  9.4 0.7 compare_select_fusion.4
  10.1 1.6 scatter_custom_fusion
  11.7 0.7 all_to_all.25
  12.4 6.0 %all-to-all-start = ((s32[32,1,16]{2,1,0:T(1,128)}), s32[32,1,16]{2,1,0:T(1,128)S(1)}, u32[]{:S(2)}, u32[]{:S(2)}) async-start(s32[32,1,16]{2,1,0:T(1,128)} %bitcast.6), calls=%async_computation | async-start | bytes 32768 | tf_op jit(solution)/shard_map/all_to_all | solution.py:58
  18.3 0.7 compare_select_fusion.3
  19.0 0.7 fusion.9
  19.7 1.2 reduce-window.16
  20.9 0.2 slice_reduce_fusion
  21.2 0.8 fusion.8
  21.9 0.7 compare_select_fusion.2
  22.6 0.1 copy.28
  22.7 0.1 reshape.157
  22.8 2.6 scatter_custom_fusion.1
  25.4 0.7 all_to_all.29
  26.1 0.0 all-to-all-done
  26.1 5.8 %all-to-all-start.2 = ((s32[32,1,32]{2,1,0:T(1,128)}), s32[32,1,32]{2,1,0:T(1,128)S(1)}, u32[]{:S(2)}, u32[]{:S(2)}) async-start(s32[32,1,32]{2,1,0:T(1,128)} %all_to_all.29), calls=%async_computation.2 | async-start | bytes 32768 | tf_op jit(solution)/shard_map/all_to_all | solution.py:65
  32.0 0.1 reshape.141
  32.0 4.5 gather_fusion
  36.6 0.0 all-to-all-done.2
  36.6 5.8 %all-to-all-start.1 = ((bf16[32,16,512]{2,1,0:T(8,128)(2,1)}), bf16[32,16,512]{2,1,0:T(8,128)(2,1)S(1)}, u32[]{:S(2)}, u32[]{:S(2)}) async-start(bf16[32,16,512]{2,1,0:T(8,128)(2,1)} %bitcast.8), calls=%async_computation.1 | async-start | bytes 1048576 | tf_op jit(solution)/shard_map/all_to_all | solution.py:75
  42.4 0.0 copy-done.4
  42.4 2.8 convert_reduce_fusion
  45.3 0.1 reshape.165
  45.3 10.5 %all-to-all-done.1 = bf16[32,16,512]{2,1,0:T(8,128)(2,1)S(1)} async-done(((bf16[32,16,512]{2,1,0:T(8,128)(2,1)}), bf16[32,16,512]{2,1,0:T(8,128)(2,1)S(1)}, u32[]{:S(2)}, u32[]{:S(2)}) %all-to-all-start.1) | async-done | bytes 524320 | tf_op jit(solution)/shard_map/all_to_all | solution.py:75
  55.8 1.2 gather_fusion.1
  57.0 1.8 pad_maximum_fusion.1
  58.8 8.1 %gather_fusion.2 = bf16[128,128,512]{2,1,0:T(8,128)(2,1)} fusion(bf16[18,128,512]{2,1,0:T(8,128)(2,1)S(1)} %pad_maximum_fusion.1, s32[1024]{0:T(1024)S(1)} %pad_clamp_fusion.1), kind=kCustom, calls=%fused_computation.2 | custom fusion | bytes 33554944 | tf_op jit(solution)/shard_map/gather | solution.py:83
  66.9 8.8 %fusion.1 = f32[16,512,128]{1,2,0:T(8,128)S(1)} fusion(bf16[16,8,128,128]{3,2,1,0:T(8,128)(2,1)} %param.17, bf16[16,8,128,512]{3,2,1,0:T(8,128)(2,1)} %bitcast.87, f32[16,128]{1,0:T(8,128)S(1)} %convert_reduce_fusion), kind=kOutput, calls=%fused_computation.16 | convolution fusion | flops 2149580800 | bytes 25174016 | tf_op jit(solution)/shard_map/rkij,rkjc->ric/dot_general | solution.py:82
  75.7 0.0 copy-done.3
  75.7 1.6 fusion
  77.3 0.0 copy-start
  77.3 5.1 %gather_fusion.5 = bf16[1024,512]{1,0:T(8,128)(2,1)} fusion(bf16[2048,512]{1,0:T(8,128)(2,1)S(1)} %fusion, s32[1024]{0:T(1024)S(1)} %broadcast_clamp_fusion), kind=kCustom, calls=%fused_computation.5 | custom fusion | bytes 2101248 | tf_op jit(solution)/shard_map/gather | solution.py:94
  82.4 0.0 copy-done
  82.4 5.2 %all-to-all-start.4 = ((bf16[32,32,512]{2,1,0:T(8,128)(2,1)}), bf16[32,32,512]{2,1,0:T(8,128)(2,1)S(1)}, u32[]{:S(2)}, u32[]{:S(2)}) async-start(bf16[32,32,512]{2,1,0:T(8,128)(2,1)} %bitcast.90), calls=%async_computation.4 | async-start | bytes 2097152 | tf_op jit(solution)/shard_map/all_to_all | solution.py:93
  87.6 8.8 %gather_fusion.3 = bf16[1024,1024]{1,0:T(8,128)(2,1)} fusion(bf16[2048,1024]{1,0:T(8,128)(2,1)} %param.15, s32[1024]{0:T(1024)S(1)} %broadcast_clamp_fusion), kind=kCustom, calls=%fused_computation.3 | custom fusion | bytes 4198400 | tf_op jit(solution)/shard_map/gather | solution.py:76
  96.3 15.4 %all-to-all-done.4 = bf16[32,32,512]{2,1,0:T(8,128)(2,1)S(1)} async-done(((bf16[32,32,512]{2,1,0:T(8,128)(2,1)}), bf16[32,32,512]{2,1,0:T(8,128)(2,1)S(1)}, u32[]{:S(2)}, u32[]{:S(2)}) %all-to-all-start.4) | async-done | bytes 1048608 | tf_op jit(solution)/shard_map/all_to_all | solution.py:93
  111.8 5.6 %all-to-all-start.3 = ((bf16[32,32,1024]{2,1,0:T(8,128)(2,1)}), bf16[32,32,1024]{2,1,0:T(8,128)(2,1)S(1)}, u32[]{:S(2)}, u32[]{:S(2)}) async-start(bf16[32,32,1024]{2,1,0:T(8,128)(2,1)} %bitcast.89), calls=%async_computation.3 | async-start | bytes 4194304 | tf_op jit(solution)/shard_map/all_to_all | solution.py:76
  117.4 0.2 reduce-scatter.2.cloned.1.call-start
  117.7 2.6 gather_fusion.6
  120.3 1.3 copy.30
  121.5 0.2 fusion.3
  121.7 41.9 %all-to-all-done.3 = bf16[32,32,1024]{2,1,0:T(8,128)(2,1)S(1)} async-done(((bf16[32,32,1024]{2,1,0:T(8,128)(2,1)}), bf16[32,32,1024]{2,1,0:T(8,128)(2,1)S(1)}, u32[]{:S(2)}, u32[]{:S(2)}) %all-to-all-start.3) | async-done | bytes 2097184 | tf_op jit(solution)/shard_map/all_to_all | solution.py:76
  163.6 2.8 gather_fusion.4
  166.4 8.4 %tanh_convert_fusion = bf16[512,4096]{1,0:T(8,128)(2,1)S(1)} fusion(bf16[512,1024]{1,0:T(8,128)(2,1)} %gather_fusion.4, bf16[4096,1024]{1,0:T(8,128)(2,1)} %param.22), kind=kOutput, calls=%fused_computation.11 | convolution fusion | flops 4297064448 | bytes 13631488 | tf_op jit(solution)/shard_map/dot_general | solution.py:27
  174.8 0.0 copy-done.5
  174.8 0.0 copy-start.1
  174.8 2.5 multiply_reduce_fusion
  177.3 0.0 copy-done.1
  177.3 0.0 copy-start.2
  177.3 5.6 %fusion.5 = f32[4096,512]{0,1:T(8,128)} fusion(bf16[512,4096]{1,0:T(8,128)(2,1)S(1)} %tanh_convert_fusion, f32[512,512]{0,1:T(8,128)S(1)} %get-tuple-element.17), kind=kOutput, calls=%fused_computation.26 | convolution fusion | flops 2148007936 | bytes 13631488 | tf_op jit(solution)/shard_map/dot_general | solution.py:21
  182.8 12.9 %fusion.4 = f32[4096,1024]{0,1:T(8,128)} fusion(bf16[512,1024]{1,0:T(8,128)(2,1)S(1)} %copy-done.2, bf16[512,4096]{1,0:T(8,128)(2,1)} %copy-done.1, bf16[4096,512]{1,0:T(8,128)(2,1)} %param.23, f32[512,512]{0,1:T(8,128)S(1)} %get-tuple-element.17), kind=kOutput, calls=%fused_computation.25 | convolution fusion | flops 6453460992 | bytes 27262976 | tf_op jit(solution)/shard_map/dot_general | solution.py:21
  195.7 18.7 %pad_maximum_fusion = f32[4096,1536]{0,1:T(8,128)} fusion(f32[4096,512]{0,1:T(8,128)} %fusion.5, f32[4096,1024]{0,1:T(8,128)} %fusion.4), kind=kLoop, calls=%fused_computation.9 | loop fusion | flops 6291456 | bytes 50331648 | tf_op jit(solution)/shard_map/concatenate | solution.py:108
  214.4 0.0 reduce-scatter.2.cloned.1.call-update
  214.4 0.6 broadcast_multiply_fusion
  215.0 242.8 %reduce-scatter.2.cloned.1.call-done = f32[128,1536]{0,1:T(8,128)} async-done(((f32[4096,1536]{0,1:T(8,128)}), f32[128,1536]{0,1:T(8,128)}) %reduce-scatter.2.cloned.1.call-update) | async-done | bytes 786448 | tf_op jit(solution)/shard_map/reduce_scatter | solution.py:107
  457.8 1.1 slice.40
  458.9 1.0 copy.31
  459.9 1.0 slice.41
  460.9 0.8 copy.32
  (16 shorter events, 0.1 us)
Async XLA Ops:
  7.2 35.3 %copy-start.4 = (s32[2048]{0:T(1024)S(1)}, s32[2048]{0:T(1024)}, u32[]{:S(2)}) copy-start(s32[2048]{0:T(1024)} %param.14) | copy-start | bytes 24580
  12.4 13.7 %all-to-all-start = ((s32[32,1,16]{2,1,0:T(1,128)}), s32[32,1,16]{2,1,0:T(1,128)S(1)}, u32[]{:S(2)}, u32[]{:S(2)}) async-start(s32[32,1,16]{2,1,0:T(1,128)} %bitcast.6), calls=%async_computation | async-start | bytes 32768 | tf_op jit(solution)/shard_map/all_to_all | solution.py:58
  26.1 10.5 %all-to-all-start.2 = ((s32[32,1,32]{2,1,0:T(1,128)}), s32[32,1,32]{2,1,0:T(1,128)S(1)}, u32[]{:S(2)}, u32[]{:S(2)}) async-start(s32[32,1,32]{2,1,0:T(1,128)} %all_to_all.29), calls=%async_computation.2 | async-start | bytes 32768 | tf_op jit(solution)/shard_map/all_to_all | solution.py:65
  36.6 19.3 %all-to-all-start.1 = ((bf16[32,16,512]{2,1,0:T(8,128)(2,1)}), bf16[32,16,512]{2,1,0:T(8,128)(2,1)S(1)}, u32[]{:S(2)}, u32[]{:S(2)}) async-start(bf16[32,16,512]{2,1,0:T(8,128)(2,1)} %bitcast.8), calls=%async_computation.1 | async-start | bytes 1048576 | tf_op jit(solution)/shard_map/all_to_all | solution.py:75
  66.9 8.8 %copy-start.3 = (s32[2048]{0:T(1024)S(1)}, s32[2048]{0:T(1024)}, u32[]{:S(2)}) copy-start(s32[2048]{0:T(1024)} %param.13) | copy-start | bytes 24580
  77.3 5.1 %copy-start = (bf16[2048,512]{1,0:T(8,128)(2,1)}, bf16[2048,512]{1,0:T(8,128)(2,1)S(1)}, u32[]{:S(2)}) copy-start(bf16[2048,512]{1,0:T(8,128)(2,1)S(1)} %fusion) | copy-start | bytes 6291460
  82.4 29.4 %all-to-all-start.4 = ((bf16[32,32,512]{2,1,0:T(8,128)(2,1)}), bf16[32,32,512]{2,1,0:T(8,128)(2,1)S(1)}, u32[]{:S(2)}, u32[]{:S(2)}) async-start(bf16[32,32,512]{2,1,0:T(8,128)(2,1)} %bitcast.90), calls=%async_computation.4 | async-start | bytes 2097152 | tf_op jit(solution)/shard_map/all_to_all | solution.py:93
  111.8 51.8 %all-to-all-start.3 = ((bf16[32,32,1024]{2,1,0:T(8,128)(2,1)}), bf16[32,32,1024]{2,1,0:T(8,128)(2,1)S(1)}, u32[]{:S(2)}, u32[]{:S(2)}) async-start(bf16[32,32,1024]{2,1,0:T(8,128)(2,1)} %bitcast.89), calls=%async_computation.3 | async-start | bytes 4194304 | tf_op jit(solution)/shard_map/all_to_all | solution.py:76
  117.4 340.4 %reduce-scatter.2.cloned.1.call-start = ((), (), s32[]{:S(2)}) async-start(), calls=%async_computation.6 | async-start | bytes 25952256 | tf_op jit(solution)/shard_map/reduce_scatter | solution.py:107
  166.4 8.4 %copy-start.5 = (bf16[4096,512]{1,0:T(8,128)(2,1)S(1)}, bf16[4096,512]{1,0:T(8,128)(2,1)}, u32[]{:S(2)}) copy-start(bf16[4096,512]{1,0:T(8,128)(2,1)} %param.23) | copy-start | bytes 12582916
  174.8 2.5 copy-start.1
  177.3 5.6 %copy-start.2 = (bf16[512,1024]{1,0:T(8,128)(2,1)S(1)}, bf16[512,1024]{1,0:T(8,128)(2,1)}, u32[]{:S(2)}) copy-start(bf16[512,1024]{1,0:T(8,128)(2,1)} %gather_fusion.4) | copy-start | bytes 3145732
Sparse Core Ops, SparseCore 0:
  214.6 243.2 reduce-scatter.1
where the time goes:
time: 471 us; the launch traced here: 469 us
  waiting for transfers between devices  311 us (66%)
  local copies, waits for them, and re-layouts  44.4 us (9%)
  matrix products  38 us (8%)
  other arithmetic  32.6 us (7%)
  starting transfers between devices  28.7 us (6%)
  between operations  14.3 us (3%)
    reduce_scatter x1, waiting for transfers between devices, on_device(): lax.psum_scatter(jnp.concatenate([contract_rows(back, batch_x), contract_...  243 us
    all_to_all x1, waiting for transfers between devices, on_device(): lax.all_to_all(features[batch_wanted], 'dev', split_axis=0, concat_axis=0...  41.9 us
    concatenate x1, other arithmetic, on_device(): jnp.concatenate([contract_rows(back, batch_x), contract_rows(hidden, resi...  18.7 us
    dot_general x2, matrix products, contract_rows(): lax.dot_general(left, right, (((0,), (0,)), ((), ())), preferred_element_...  18.4 us
    all_to_all x1, waiting for transfers between devices, on_device(): lax.all_to_all(propagated[batch_wanted], 'dev', split_axis=0, concat_axis...  15.4 us
    all_to_all x1, waiting for transfers between devices, on_device(): lax.all_to_all(halo_served, 'dev', split_axis=0, concat_axis=0, tiled=True)  10.5 us
  transfers between devices with their start and end apart: 6, of which 4 were waited for; matrix products, arithmetic and copies ran while one was open for 6% of the time, Pallas kernels for 0%

commit v1 on v0

v1 whole, which is shorter than its diff:
```python
import math

import jax
import jax.numpy as jnp
from jax import lax
from jax.experimental import pallas as pl
from jax.experimental.pallas import tpu as pltpu
from jax.sharding import PartitionSpec as P


def slot_of(owner, capacity):
    row = jnp.arange(owner.shape[0], dtype=jnp.int32)
    same = (owner[:, None] == owner[None, :]) & (row[None, :] < row[:, None])
    return owner * capacity + jnp.sum(same.astype(jnp.int32), axis=1)


def request_table(position, local, capacity, devices):
    slot = jnp.arange(devices * capacity, dtype=jnp.int32)
    match = slot[:, None] == position[None, :]
    table = jnp.sum(jnp.where(match, local[None, :] + 1, 0), axis=1) - 1
    return table.reshape(devices, capacity)


def contract_rows(left, right):
    return lax.dot_general(
        left, right, (((0,), (0,)), ((), ())), preferred_element_type=jnp.float32
    )


def contract_cols(left, right):
    return lax.dot_general(
        left, right, (((1,), (1,)), ((), ())), preferred_element_type=jnp.float32
    )


def spread_kernel(cols_ref, weights_ref, own_ref, halo_ref, seed_ref, out_ref, table_ref):
    r = pl.program_id(0)
    per_row = weights_ref.shape[1]
    rows = weights_ref.shape[2]
    own = own_ref.shape[0]

    @pl.when(r == 0)
    def _():
        table_ref[:own] = own_ref[...]
        table_ref[own:] = halo_ref[...]

    total = jnp.zeros((rows, own_ref.shape[2]), jnp.float32)
    weight = jnp.zeros((rows, weights_ref.shape[3]), jnp.float32)
    for k in range(per_row):
        block = weights_ref[0, k]
        total += jnp.dot(block, table_ref[cols_ref[r, k]], preferred_element_type=jnp.float32)
        weight += block.astype(jnp.float32)
    degree = jnp.sum(weight, axis=1, keepdims=True)
    classes = lax.broadcasted_iota(jnp.int32, total.shape, 1)
    seeds = (classes == seed_ref[...]).astype(jnp.float32)
    out_ref[...] = (0.8 * (total / degree) + 0.2 * seeds).astype(out_ref.dtype)


def propagate(tile_cols, tile_weights, prior_labels, halo_labels, seed_class):
    row_tiles, per_row, rows, _ = tile_weights.shape
    node_count, classes = prior_labels.shape
    own_tiles = node_count // rows
    halo_tiles = halo_labels.shape[0] // rows
    return pl.pallas_call(
        spread_kernel,
        out_shape=jax.ShapeDtypeStruct((node_count, classes), jnp.bfloat16),
        grid_spec=pltpu.PrefetchScalarGridSpec(
            num_scalar_prefetch=1,
            grid=(row_tiles,),
            in_specs=[
                pl.BlockSpec((1, per_row, rows, rows), lambda r, c: (r, 0, 0, 0)),
                pl.BlockSpec((own_tiles, rows, classes), lambda r, c: (0, 0, 0)),
                pl.BlockSpec((halo_tiles, rows, classes), lambda r, c: (0, 0, 0)),
                pl.BlockSpec((rows, 1), lambda r, c: (r, 0)),
            ],
            out_specs=pl.BlockSpec((rows, classes), lambda r, c: (r, 0)),
            scratch_shapes=[pltpu.VMEM((own_tiles + halo_tiles, rows, classes), jnp.bfloat16)],
        ),
        compiler_params=pltpu.CompilerParams(
            dimension_semantics=("arbitrary",), vmem_limit_bytes=24 << 20
        ),
        cost_estimate=pl.CostEstimate(
            flops=2 * node_count * per_row * rows * classes,
            bytes_accessed=2 * (tile_weights.size + 2 * prior_labels.size),
            transcendentals=0,
        ),
    )(
        tile_cols,
        tile_weights,
        prior_labels.reshape(own_tiles, rows, classes),
        halo_labels.reshape(halo_tiles, rows, classes),
        seed_class[:, None],
    )


def on_device(
    prior_labels,
    label_class,
    labeled,
    features,
    tile_cols,
    tile_weights,
    halo_owner,
    halo_local,
    batch_owner,
    batch_local,
    w_in,
    w_out,
):
    devices = lax.axis_size("dev")
    chips = devices // 2
    me = lax.axis_index("dev")
    chip, core = me // 2, lax.rem(me, 2)
    swap = [(i, i ^ 1) for i in range(devices)]
    across = [[2 * i + c for i in range(chips)] for c in range(2)]

    classes = prior_labels.shape[1]
    feat_width = features.shape[1]
    hidden_units = w_in.shape[0]
    unit_block = hidden_units // devices
    halo_count = halo_owner.shape[0]
    batch_count = batch_owner.shape[0]
    halo_capacity = 2 * halo_count // devices
    batch_capacity = 2 * batch_count // devices
    slots = devices * batch_capacity

    halo_slot = slot_of(halo_owner[:, 0], halo_capacity)
    batch_slot = slot_of(batch_owner[:, 0], batch_capacity)
    asked = jnp.concatenate(
        [
            request_table(halo_slot, halo_local, halo_capacity, devices),
            request_table(batch_slot, batch_local, batch_capacity, devices),
        ],
        axis=1,
    )
    wanted = lax.all_to_all(asked, "dev", split_axis=0, concat_axis=0, tiled=True)
    halo_wanted = jnp.maximum(wanted[:, :halo_capacity], 0).reshape(-1)
    batch_asked = wanted[:, halo_capacity:].reshape(-1)
    batch_wanted = jnp.maximum(batch_asked, 0)
    halo_back = lax.all_to_all(
        prior_labels[halo_wanted].reshape(devices, halo_capacity, classes),
        "dev",
        split_axis=0,
        concat_axis=0,
        tiled=True,
    )

    w_in_half = lax.dynamic_index_in_dim(
        w_in.reshape(chips, 2, unit_block, feat_width), core, 1, keepdims=False
    ).reshape(-1, feat_width)
    w_out_half = lax.dynamic_index_in_dim(
        w_out.reshape(chips, 2, unit_block, classes), core, 1, keepdims=False
    ).reshape(-1, classes)

    def both_cores(own):
        return jnp.concatenate([own, lax.ppermute(own, "dev", swap)], axis=0)

    x = both_cores(features[batch_wanted])
    hidden = jnp.tanh(contract_cols(x, w_in_half)).astype(jnp.bfloat16)
    partial = jnp.dot(hidden, w_out_half, preferred_element_type=jnp.float32)
    logits = partial[:slots] + lax.ppermute(partial[slots:], "dev", swap)

    halo_labels = halo_back.reshape(devices * halo_capacity, classes)[halo_slot]
    seed_class = jnp.where(labeled == 1, label_class, -1)
    propagated = propagate(tile_cols, tile_weights, prior_labels, halo_labels, seed_class)

    log_z = jnp.log(propagated[batch_wanted].astype(jnp.float32))
    target = log_z - jnp.mean(log_z, axis=1, keepdims=True)
    differ = logits - target
    slot_error = 0.5 * jnp.mean(differ * differ, axis=1)
    scaled = differ / math.sqrt(batch_count * devices)
    residue_own = jnp.where((batch_asked >= 0)[:, None], scaled, 0.0).astype(jnp.bfloat16)
    residue = both_cores(residue_own)

    def over_chips(left, right):
        gradient = contract_rows(left, right).astype(jnp.bfloat16)
        own = contract_rows(lax.dynamic_slice_in_dim(left, chip * unit_block, unit_block, 1), right)
        blocks = lax.all_to_all(
            gradient.reshape(chips, unit_block, gradient.shape[1]),
            "dev",
            split_axis=0,
            concat_axis=0,
            tiled=True,
            axis_index_groups=across,
        )
        other = (jnp.arange(chips, dtype=jnp.int32) != chip)[:, None, None]
        return own + jnp.sum(jnp.where(other, blocks.astype(jnp.float32), 0.0), axis=0)

    grad_out = over_chips(hidden, residue)
    hidden_wide = hidden.astype(jnp.float32)
    back = (contract_cols(residue, w_out_half) * (1.0 - hidden_wide * hidden_wide)).astype(
        jnp.bfloat16
    )
    grad_in = over_chips(back, x)

    error_back = lax.all_to_all(
        slot_error.reshape(devices, batch_capacity),
        "dev",
        split_axis=0,
        concat_axis=0,
        tiled=True,
    ).reshape(-1)
    mine = batch_slot[:, None] == jnp.arange(slots, dtype=jnp.int32)[None, :]
    row_error = jnp.sum(jnp.where(mine, error_back[None, :], 0.0), axis=1)
    return (propagated, row_error, grad_in, grad_out)


def solution(mesh):
    in_specs = (
        P("dev", None),
        P("dev"),
        P("dev"),
        P("dev", None),
        P("dev", None),
        P("dev", None, None, None),
        P("dev", None),
        P("dev"),
        P("dev", None),
        P("dev"),
        P(),
        P(),
    )
    out_specs = (P("dev", None), P("dev"), P("dev", None), P("dev", None))
    return jax.shard_map(
        on_device, mesh=mesh, in_specs=in_specs, out_specs=out_specs, check_vma=False
    )
```

time: 471 us -> 271 us (0.58)
  waiting for transfers between devices: 311 us -> 123 us
  other arithmetic: 32.6 us -> 12.8 us
  matrix products: 38 us -> 54.3 us
  between operations: 14.3 us -> 0.98 us
  local copies, waits for them, and re-layouts: 44.4 us -> 33.9 us
  Pallas kernels: 0 us -> 10 us
  blocking collectives: 0 us -> 9.99 us
    reduce_scatter x1 -> x0, waiting for transfers between devices: 243 us -> none  [on_device(): lax.psum_scatter(jnp.concatenate([contract_rows(back, batch_x), contract_...]
    all_to_all x5 -> x4, waiting for transfers between devices: 67.8 us -> 123 us  [the longest x2 110 us: over_chips(): lax.all_to_all(gradient.reshape(chips, unit_block, gradient.shape[1]), 'd...]
    concatenate x2 -> x1, other arithmetic: 20.5 us -> 0.08 us  [on_device(): jnp.concatenate([request_table(halo_slot, halo_local, halo_capacity, devi...]
    gather x7 -> x3, local copies, waits for them, and re-layouts: 33.1 us -> 16.2 us  [the longest x1 7.71 us: on_device(): x = both_cores(features[batch_wanted])]
    dot_general x1 -> x2, matrix products: 8.39 us -> 21.8 us  [contract_cols(): lax.dot_general(left, right, (((1,), (1,)), ((), ())), preferred_element_...]
    pallas_call x0 -> x1, Pallas kernels: none -> 10 us  [propagate(): pl.pallas_call(spread_kernel, out_shape=jax.ShapeDtypeStruct((node_count,...]
    all_to_all x0 -> x1, blocking collectives: none -> 9.99 us  [on_device(): lax.all_to_all(asked, 'dev', split_axis=0, concat_axis=0, tiled=True)]
    dot_general x2 -> x4, matrix products: 18.4 us -> 28 us  [contract_rows(): lax.dot_general(left, right, (((0,), (0,)), ((), ())), preferred_element_...]
  transfers between devices with their start and end apart: 6 -> 7, of which waited for: 4 -> 3; matrix products, arithmetic and copies ran while one was open for 6% -> 22% of each run, Pallas kernels for 0% -> 4%
where the time goes in v1:
time: 271 us; the launch traced here: 270 us
  waiting for transfers between devices  123 us (45%)
  matrix products  54.3 us (20%)
  local copies, waits for them, and re-layouts  33.9 us (13%)
  starting transfers between devices  24.2 us (9%)
  other arithmetic  12.8 us (5%)
  Pallas kernels  10 us (4%)
  blocking collectives  9.99 us (4%)
    all_to_all x2, waiting for transfers between devices, over_chips(): lax.all_to_all(gradient.reshape(chips, unit_block, gradient.shape[1]), 'd...  110 us
    dot_general x4, matrix products, contract_rows(): lax.dot_general(left, right, (((0,), (0,)), ((), ())), preferred_element_...  28 us
    dot_general x2, matrix products, contract_cols(): lax.dot_general(left, right, (((1,), (1,)), ((), ())), preferred_element_...  21.8 us
    all_to_all x1, waiting for transfers between devices, on_device(): lax.all_to_all(prior_labels[halo_wanted].reshape(devices, halo_capacity,...  12.8 us
    all_to_all x2, starting transfers between devices, over_chips(): lax.all_to_all(gradient.reshape(chips, unit_block, gradient.shape[1]), 'd...  12.3 us
    pallas_call x1, Pallas kernels, propagate(): pl.pallas_call(spread_kernel, out_shape=jax.ShapeDtypeStruct((node_count,...  10 us
    all_to_all x1, blocking collectives, on_device(): lax.all_to_all(asked, 'dev', split_axis=0, concat_axis=0, tiled=True)  9.99 us
    gather x1, local copies, waits for them, and re-layouts, on_device(): x = both_cores(features[batch_wanted])  7.71 us
  transfers between devices with their start and end apart: 7, of which 3 were waited for; matrix products, arithmetic and copies ran while one was open for 22% of the time, Pallas kernels for 4%

profile of v1, /device:TPU:14, one launch (start us, length us, event | category | flops | bytes accessed | tf_op | source)
XLA Modules:
  0.0 269.6 jit_solution(8877016518677206760)
XLA Ops:
  0.6 1.0 convert_reduce_fusion
  1.6 0.7 multiply_add_fusion.1
  2.3 0.3 select_reduce_fusion.3
  2.6 0.1 sub.36
  2.7 0.9 convert_reduce_fusion.1
  3.6 0.7 multiply_add_fusion.2
  4.4 0.1 select_reduce_fusion.4
  4.5 0.1 sub.34
  4.6 0.1 pad_add_fusion
  4.7 10.0 %all_to_all.33 = s32[32,1,48]{2,1,0:T(1,128)S(1)} all-to-all(s32[32,1,48]{2,1,0:T(1,128)S(1)} %bitcast.41), channel_id=1, replica_groups=mesh['dev'=32] {'dev'}, dimensions={0} | all-to-all | bytes 12288 | tf_op jit(solution)/shard_map/all_to_all | solution.py:136
  14.7 0.1 slice_maximum_fusion.1
  14.7 0.1 reshape.180
  14.8 7.7 %gather_fusion.2 = bf16[1024,1024]{1,0:T(8,128)(2,1)S(1)} fusion(bf16[2048,1024]{1,0:T(8,128)(2,1)} %param.15, s32[1024]{0:T(1024)S(1)} %broadcast_clamp_fusion), kind=kCustom, calls=%fused_computation.2 | custom fusion | bytes 4198400 | tf_op jit(solution)/shard_map/gather | solution.py:158
  22.5 0.1 collective-permute-start
  22.6 1.8 constant_dynamic-slice_fusion
  24.4 3.7 %constant_dynamic-slice_fusion.1 = bf16[16,1,128,1024]{3,2,1,0:T(8,128)(2,1)S(1)} fusion(bf16[16,2,128,1024]{3,2,1,0:T(8,128)(2,1)} %bitcast.33, s32[]{:T(128)S(6)} %select_n.64), kind=kLoop, calls=%fused_computation.54 | loop fusion | bytes 8388612 | tf_op jit(solution)/shard_map/jit(dynamic_index_in_dim)/dynamic_slice | solution.py:148
  28.1 0.2 constant_dynamic-update-slice_fusion.1
  28.3 0.0 collective-permute-done
  28.3 1.8 constant_dynamic-update-slice_fusion
  30.1 0.0 copy-start.2
  30.1 9.4 %tanh_convert_fusion = bf16[2048,2048]{1,0:T(8,128)(2,1)S(1)} fusion(bf16[2048,1024]{1,0:T(8,128)(2,1)S(1)} %constant_dynamic-update-slice_fusion, bf16[2048,1024]{1,0:T(8,128)(2,1)S(1)} %bitcast.32), kind=kOutput, calls=%fused_computation.5 | convolution fusion | flops 8594128896 | bytes 16777216 | tf_op jit(solution)/shard_map/dot_general | solution.py:31
  39.5 0.0 copy-done.2
  39.5 0.0 copy-start.13
  39.5 4.5 %fusion.11 = f32[2048,512]{1,0:T(8,128)S(1)} fusion(bf16[2048,2048]{1,0:T(8,128)(2,1)S(1)} %tanh_convert_fusion, bf16[2048,512]{1,0:T(8,128)(2,1)S(1)} %bitcast.34), kind=kOutput, calls=%fused_computation.62 | convolution fusion | flops 4294967296 | bytes 14680064 | tf_op jit(solution)/shard_map/dot_general | solution.py:160
  44.0 2.0 copy-done.5
  46.0 1.5 slice.27
  47.5 0.5 collective-permute-start.1
  48.0 0.1 reshape.152
  48.1 0.3 copy-done
  48.4 2.6 gather_fusion
  51.0 6.2 %all-to-all-start.1 = ((bf16[32,16,512]{2,1,0:T(8,128)(2,1)}), bf16[32,16,512]{2,1,0:T(8,128)(2,1)}, u32[]{:S(2)}, u32[]{:S(2)}) async-start(bf16[32,16,512]{2,1,0:T(8,128)(2,1)} %bitcast.6), calls=%async_computation.1 | async-start | bytes 1048576 | tf_op jit(solution)/shard_map/all_to_all | solution.py:140
  57.2 0.4 copy.22.seed_ref
  57.6 0.1 copy.21.cols_ref
  57.7 0.1 slice_compare_fusion
  57.8 0.1 ge.11
  57.8 12.8 %all-to-all-done.1 = bf16[32,16,512]{2,1,0:T(8,128)(2,1)} async-done(((bf16[32,16,512]{2,1,0:T(8,128)(2,1)}), bf16[32,16,512]{2,1,0:T(8,128)(2,1)}, u32[]{:S(2)}, u32[]{:S(2)}) %all-to-all-start.1) | async-done | bytes 524320 | tf_op jit(solution)/shard_map/all_to_all | solution.py:140
  70.7 2.3 gather_fusion.1
  73.0 0.0 copy-start.1
  73.0 2.2 copy-done.1
  75.2 10.0 %shard_map.147 = bf16[2048,512]{1,0:T(8,128)(2,1)} custom-call(s32[16,8]{1,0:T(8,128)S(1)} %copy.21.cols_ref, bf16[16,8,128,128]{3,2,1,0:T(8,128)(2,1)S(1)} %copy-done.1, bf16[16,128,512]{2,1,0:T(8,128)(2,1)S(1)} %bitcast.29, bf16[2,128,512]{2,1,0:T(8,128)(2,1)S(1)} %bitcast.30, s32[2048,1]{1,0:T(8,128)S(1)} %copy.22.seed_ref), custom_call_target="tpu_custom_call" | custom-call | flops 2147483648 | bytes 8388608 | tf_op jit(solution)/shard_map/pallas_call | solution.py:64
  85.2 5.8 %gather_fusion.3 = bf16[1024,512]{1,0:T(8,128)(2,1)S(1)} fusion(bf16[2048,512]{1,0:T(8,128)(2,1)} %shard_map.147, s32[1024]{0:T(1024)S(1)} %broadcast_clamp_fusion), kind=kCustom, calls=%fused_computation.3 | custom fusion | bytes 2101248 | tf_op jit(solution)/shard_map/gather | solution.py:167
  91.1 0.4 fusion.1
  91.4 0.0 collective-permute-done.1
  91.5 2.8 %select_convert_fusion = (bf16[1024,512]{1,0:T(8,128)(2,1)S(1)}, f32[1024]{0:T(1024)S(1)}) fusion(pred[1024]{0:T(1024)(128)(4,1)S(1)} %ge.11, f32[1024]{0:T(1024)S(1)} %broadcast_multiply_fusion.1, bf16[1024,512]{1,0:T(8,128)(2,1)S(1)} %gather_fusion.3, f32[1024,512]{1,0:T(8,128)} %collective-permute-done.1, f32[2048,512]{1,0:T(8,128)} %copy-done.5), kind=kLoop, calls=%fused_computation.13 | loop fusion | flops 4717568 | bytes 6300672 | tf_op jit(solution)/shard_map/convert_element_type | solution.py:172
  94.3 0.1 collective-permute-start.2
  94.4 0.7 mul.71
  95.1 5.1 %all-to-all-start.2 = ((f32[32,1,32]{2,1,0:T(1,128)}), f32[32,1,32]{2,1,0:T(1,128)S(1)}, u32[]{:S(2)}, u32[]{:S(2)}) async-start(f32[32,1,32]{2,1,0:T(1,128)} %mul.71), calls=%async_computation.2 | async-start | bytes 32768 | tf_op jit(solution)/shard_map/all_to_all | solution.py:196
  100.2 0.0 collective-permute-done.2
  100.2 9.9 %convolution_convert_fusion.1 = bf16[2048,512]{1,0:T(8,128)(2,1)} fusion(bf16[2048,2048]{1,0:T(8,128)(2,1)} %copy-done.13, bf16[1024,512]{1,0:T(8,128)(2,1)S(1)} %collective-permute-done.2, bf16[1024,512]{1,0:T(8,128)(2,1)S(1)} %get-tuple-element.4), kind=kOutput, calls=%fused_computation.9 | convolution fusion | flops 4300210176 | bytes 12582912 | tf_op jit(solution)/shard_map/dot_general | solution.py:25
  110.1 0.0 all-to-all-done.2
  110.1 7.0 %all-to-all-start.4 = ((bf16[16,128,512]{2,1,0:T(8,128)(2,1)}), bf16[16,128,512]{2,1,0:T(8,128)(2,1)S(1)}, u32[]{:S(2)}, u32[]{:S(2)}) async-start(bf16[16,128,512]{2,1,0:T(8,128)(2,1)} %bitcast.36), calls=%async_computation.4 | async-start | bytes 4194304 | tf_op jit(solution)/shard_map/all_to_all | solution.py:178
  117.1 12.4 %multiply_convert_fusion = bf16[2048,2048]{1,0:T(8,128)(2,1)} fusion(bf16[2048,2048]{1,0:T(8,128)(2,1)} %copy-done.13, bf16[2048,512]{1,0:T(8,128)(2,1)} %bitcast.35, bf16[1024,512]{1,0:T(8,128)(2,1)} %copy-done.12, bf16[1024,512]{1,0:T(8,128)(2,1)S(1)} %get-tuple-element.4), kind=kOutput, calls=%fused_computation.4 | convolution fusion | flops 4320133120 | bytes 20971520 | tf_op jit(solution)/shard_map/dot_general | solution.py:31
  129.6 12.9 %convolution_convert_fusion = bf16[2048,1024]{1,0:T(8,128)(2,1)} fusion(bf16[2048,2048]{1,0:T(8,128)(2,1)} %multiply_convert_fusion, bf16[2048,1024]{1,0:T(8,128)(2,1)S(1)} %copy-done.3), kind=kOutput, calls=%fused_computation.8 | convolution fusion | flops 8592031744 | bytes 16777216 | tf_op jit(solution)/shard_map/dot_general | solution.py:25
  142.5 22.9 %all-to-all-done.4 = bf16[16,128,512]{2,1,0:T(8,128)(2,1)S(1)} async-done(((bf16[16,128,512]{2,1,0:T(8,128)(2,1)}), bf16[16,128,512]{2,1,0:T(8,128)(2,1)S(1)}, u32[]{:S(2)}, u32[]{:S(2)}) %all-to-all-start.4) | async-done | bytes 2097184 | tf_op jit(solution)/shard_map/all_to_all | solution.py:178
  165.4 5.2 %all-to-all-start.3 = ((bf16[16,128,1024]{2,1,0:T(8,128)(2,1)}), bf16[16,128,1024]{2,1,0:T(8,128)(2,1)}, u32[]{:S(2)}, u32[]{:S(2)}) async-start(bf16[16,128,1024]{2,1,0:T(8,128)(2,1)} %bitcast.31), calls=%async_computation.3 | async-start | bytes 8388608 | tf_op jit(solution)/shard_map/all_to_all | solution.py:178
  170.7 0.5 broadcast.110
  171.2 0.7 reduce.3
  171.9 0.1 broadcast_in_dim.107
  172.0 0.9 select_reduce_fusion.2
  172.9 0.5 select_reduce_fusion.1
  173.4 2.6 convolution_add_fusion.1
  176.0 87.6 %all-to-all-done.3 = bf16[16,128,1024]{2,1,0:T(8,128)(2,1)} async-done(((bf16[16,128,1024]{2,1,0:T(8,128)(2,1)}), bf16[16,128,1024]{2,1,0:T(8,128)(2,1)}, u32[]{:S(2)}, u32[]{:S(2)}) %all-to-all-start.3) | async-done | bytes 4194336 | tf_op jit(solution)/shard_map/all_to_all | solution.py:178
  263.6 3.5 %select_reduce_fusion = f32[128,1024]{1,0:T(8,128)S(1)} fusion(bf16[16,128,1024]{2,1,0:T(8,128)(2,1)} %all-to-all-done.3, pred[16]{0:T(512)(128)(4,1)S(1)} %iota_compare_fusion.5), kind=kLoop, calls=%fused_computation.6 | loop fusion | flops 6160384 | bytes 4718608 | tf_op jit(solution)/shard_map/reduce_sum | solution.py:187
  267.1 2.6 convolution_add_fusion
  (34 shorter events, 0.1 us)
Async XLA Ops:
  22.5 5.8 %collective-permute-start = (bf16[1024,1024]{1,0:T(8,128)(2,1)S(1)}, bf16[1024,1024]{1,0:T(8,128)(2,1)}, u32[]{:S(2)}, u32[]{:S(2)}) collective-permute-start(bf16[1024,1024]{1,0:T(8,128)(2,1)S(1)} %gather_fusion.2), channel_id=1, source_target_pairs={{0,1},{1,0},{2,3},{3,2},{4,5},{5,4},{6,7},{7,6},{8,9},{9,8},{10,11... | collective-permute-start | bytes 6291464 | tf_op jit(solution)/shard_map/ppermute | solution.py:156
  24.4 15.1 %copy-start.6 = (bf16[16,1,128,512]{3,2,1,0:T(8,128)(2,1)}, bf16[16,1,128,512]{3,2,1,0:T(8,128)(2,1)S(1)}, u32[]{:S(2)}) copy-start(bf16[16,1,128,512]{3,2,1,0:T(8,128)(2,1)S(1)} %constant_dynamic-slice_fusion) | copy-start | bytes 6291460
  30.1 9.4 %copy-start.2 = (bf16[2048,1024]{1,0:T(8,128)(2,1)}, bf16[2048,1024]{1,0:T(8,128)(2,1)S(1)}, u32[]{:S(2)}) copy-start(bf16[2048,1024]{1,0:T(8,128)(2,1)S(1)} %constant_dynamic-update-slice_fusion) | copy-start | bytes 12582916
  39.5 4.6 %copy-start.13 = (bf16[2048,2048]{1,0:T(8,128)(2,1)}, bf16[2048,2048]{1,0:T(8,128)(2,1)S(1)}, u32[]{:S(2)}) copy-start(bf16[2048,2048]{1,0:T(8,128)(2,1)S(1)} %tanh_convert_fusion) | copy-start | bytes 25165828
  44.0 2.0 copy-start.5
  46.0 2.3 copy-start
  46.0 11.2 %copy-start.9 = (s32[2048]{0:T(1024)S(1)}, s32[2048]{0:T(1024)}, u32[]{:S(2)}) copy-start(s32[2048]{0:T(1024)} %param.13) | copy-start | bytes 24580
  46.0 11.2 %copy-start.10 = (s32[2048]{0:T(1024)S(1)}, s32[2048]{0:T(1024)}, u32[]{:S(2)}) copy-start(s32[2048]{0:T(1024)} %param.14) | copy-start | bytes 24580
  47.5 10.1 %copy-start.11 = (s32[16,8]{0,1:T(8,128)S(1)}, s32[16,8]{0,1:T(8,128)}, u32[]{:S(2)}) copy-start(s32[16,8]{0,1:T(8,128)} %param.16) | copy-start | bytes 1540
  47.5 10.1 %copy-start.8 = (s32[256,1]{0,1:T(1,128)S(1)}, s32[256,1]{0,1:T(1,128)}, u32[]{:S(2)}) copy-start(s32[256,1]{0,1:T(1,128)} %param.18) | copy-start | bytes 3076
  47.5 43.9 %collective-permute-start.1 = (f32[1024,512]{1,0:T(8,128)}, f32[1024,512]{1,0:T(8,128)}, u32[]{:S(2)}, u32[]{:S(2)}) collective-permute-start(f32[1024,512]{1,0:T(8,128)} %slice.27), channel_id=1, source_target_pairs={{0,1},{1,0},{2,3},{3,2},{4,5},{5,4},{6,7},{7,6},{8,9},{9,8},{10,11... | collective-permute-start | bytes 6291464 | tf_op jit(solution)/shard_map/ppermute | solution.py:161
  51.0 19.7 %all-to-all-start.1 = ((bf16[32,16,512]{2,1,0:T(8,128)(2,1)}), bf16[32,16,512]{2,1,0:T(8,128)(2,1)}, u32[]{:S(2)}, u32[]{:S(2)}) async-start(bf16[32,16,512]{2,1,0:T(8,128)(2,1)} %bitcast.6), calls=%async_computation.1 | async-start | bytes 1048576 | tf_op jit(solution)/shard_map/all_to_all | solution.py:140
  73.0 2.2 copy-start.1
  94.3 5.9 %collective-permute-start.2 = (bf16[1024,512]{1,0:T(8,128)(2,1)S(1)}, bf16[1024,512]{1,0:T(8,128)(2,1)S(1)}, u32[]{:S(2)}, u32[]{:S(2)}) collective-permute-start(bf16[1024,512]{1,0:T(8,128)(2,1)S(1)} %get-tuple-element.4), channel_id=1, source_target_pairs={{0,1},{1,0},{2,3},{3,2},{4,5},{5,4},{6,7},{7,6},{8,9},{9,8},{10,11... | collective-permute-start | bytes 3145736 | tf_op jit(solution)/shard_map/ppermute | solution.py:156
  95.1 15.1 %all-to-all-start.2 = ((f32[32,1,32]{2,1,0:T(1,128)}), f32[32,1,32]{2,1,0:T(1,128)S(1)}, u32[]{:S(2)}, u32[]{:S(2)}) async-start(f32[32,1,32]{2,1,0:T(1,128)} %mul.71), calls=%async_computation.2 | async-start | bytes 32768 | tf_op jit(solution)/shard_map/all_to_all | solution.py:196
  100.2 9.9 %copy-start.12 = (bf16[1024,512]{1,0:T(8,128)(2,1)}, bf16[1024,512]{1,0:T(8,128)(2,1)S(1)}, u32[]{:S(2)}) copy-start(bf16[1024,512]{1,0:T(8,128)(2,1)S(1)} %collective-permute-done.2) | copy-start | bytes 3145732
  110.1 55.3 %all-to-all-start.4 = ((bf16[16,128,512]{2,1,0:T(8,128)(2,1)}), bf16[16,128,512]{2,1,0:T(8,128)(2,1)S(1)}, u32[]{:S(2)}, u32[]{:S(2)}) async-start(bf16[16,128,512]{2,1,0:T(8,128)(2,1)} %bitcast.36), calls=%async_computation.4 | async-start | bytes 4194304 | tf_op jit(solution)/shard_map/all_to_all | solution.py:178
  117.1 12.4 %copy-start.3 = (bf16[2048,1024]{1,0:T(8,128)(2,1)S(1)}, bf16[2048,1024]{1,0:T(8,128)(2,1)}, u32[]{:S(2)}) copy-start(bf16[2048,1024]{1,0:T(8,128)(2,1)} %copy-done.2) | copy-start | bytes 12582916
  165.4 5.3 %copy-start.7 = (s32[512,1]{0,1:T(1,128)S(1)}, s32[512,1]{0,1:T(1,128)}, u32[]{:S(2)}) copy-start(s32[512,1]{0,1:T(1,128)} %param.20) | copy-start | bytes 6148
  165.4 98.1 %all-to-all-start.3 = ((bf16[16,128,1024]{2,1,0:T(8,128)(2,1)}), bf16[16,128,1024]{2,1,0:T(8,128)(2,1)}, u32[]{:S(2)}, u32[]{:S(2)}) async-start(bf16[16,128,1024]{2,1,0:T(8,128)(2,1)} %bitcast.31), calls=%async_computation.3 | async-start | bytes 8388608 | tf_op jit(solution)/shard_map/all_to_all | solution.py:178
  263.6 3.5 %copy-start.4 = (bf16[2048,1024]{1,0:T(8,128)(2,1)S(1)}, bf16[2048,1024]{1,0:T(8,128)(2,1)}, u32[]{:S(2)}) copy-start(bf16[2048,1024]{1,0:T(8,128)(2,1)} %copy-done.2) | copy-start | bytes 12582916
